TPU v7x, 32 devices: a whole 2x2x4 slice. The times are simulated.
32 devices in a mesh: space: 16 (over z, x, core), chan: 2 (over y).
Axes of the slice: x: 2, y: 2, z: 4, core: 2. Of those that a mesh axis runs over, the one named last changes fastest.
Arguments:
- volume: bfloat16 [256, 16, 8, 128], P('chan', 'space'), may hold values from -6 to 6
- w_first: bfloat16 [256, 27, 256], P(None, None, 'chan'), may hold values from -0.078125 to 0.078125
- b_first: float32 [256], P('chan'), may hold values from -1.8 to 1.8
- w_second: bfloat16 [256, 27, 256], P('chan'), may hold values from -0.125 to 0.125
- b_second: float32 [256], P('chan'), may hold values from -1.8 to 1.8
Outputs:
- result: bfloat16 [256, 16, 8, 128], P('chan', 'space')
All inputs are finite; a program needn't handle non-finite values.
Results may differ from a plain program's by a relative error of at most 0.011.
Values may be sent and summed in bfloat16 or wider, within the bound.
No kernel may reach another device: no remote copies, remote signals or barrier semaphores. Data moves between devices by JAX's collectives and lax.ppermute only.
A program may use at most 64 MiB of HBM per device.

v0:
```python
import jax
import jax.numpy as jnp
from jax import lax
from jax.sharding import PartitionSpec as P


def with_halo(cells, sides, width):
    for axis, dim in sides:
        count = lax.axis_size(axis)
        ends = count - 1
        head = lax.slice_in_dim(cells, 0, width, axis=dim)
        tail = lax.slice_in_dim(cells, cells.shape[dim] - width, cells.shape[dim], axis=dim)
        cells = jnp.concatenate(
            [
                lax.ppermute(tail, axis, [(i, (i + 1) % count) for i in range(ends)]),
                cells,
                lax.ppermute(head, axis, [((i + 1) % count, i) for i in range(ends)]),
            ],
            axis=dim,
        )
    return cells


def apply_taps(slab, weights, row_pad):
    kernel = weights.reshape(weights.shape[0], 3, 3, 3, weights.shape[2])
    summed = lax.conv_general_dilated(
        slab[None],
        kernel,
        (1, 1, 1),
        [(0, 0), (row_pad, row_pad), (1, 1)],
        dimension_numbers=("NCDHW", "IDHWO", "NCDHW"),
        preferred_element_type=jnp.float32,
    )
    return summed[0]


def per_device(volume, w_first, b_first, w_second, b_second):
    gathered = lax.all_gather(volume, "chan", axis=0, tiled=True)
    framed = with_halo(gathered, (("space", 1),), 1)
    first_sum = apply_taps(framed, w_first, 1)
    hidden = jax.nn.relu(first_sum + b_first[:, None, None, None]).astype(jnp.bfloat16)
    beside_all = with_halo(hidden, (("space", 1),), 1)
    second_sum = lax.psum_scatter(
        apply_taps(beside_all, w_second, 1).astype(jnp.bfloat16),
        "chan",
        scatter_dimension=0,
        tiled=True,
    ).astype(jnp.float32)
    return jax.nn.relu(second_sum + b_second[:, None, None, None]).astype(jnp.bfloat16)


def solution(mesh):
    in_specs = (
        P("chan", "space", None, None),
        P(None, None, "chan"),
        P("chan"),
        P("chan", None, None),
        P("chan"),
    )
    out_specs = P("chan", "space", None, None)
    return jax.shard_map(
        per_device, mesh=mesh, in_specs=in_specs, out_specs=out_specs, check_vma=False
    )
```

profile of v0, /device:TPU:0, one launch (start us, length us, event | category | flops | bytes accessed | tf_op | source)
XLA Modules:
  0.0 113.9 jit_solution(8084966245108863844)
XLA Ops:
  6.5 0.0 copy-start
  6.5 0.0 reduce-scatter.4.cloned.1.call-start
  6.5 1.3 %copy.15 = bf16[128,1,8,128]{0,2,3,1:T(8,128)(2,1)S(1)} copy(bf16[128,1,8,128]{3,2,1,0:T(8,128)(2,1)} %param.5) | data formatting | bytes 524288 | tf_op args[0]
  7.9 10.0 %all_gather.3 = bf16[256,1,8,128]{0,2,3,1:T(8,128)(2,1)S(1)} all-gather(bf16[128,1,8,128]{0,2,3,1:T(8,128)(2,1)S(1)} %copy.15), channel_id=1, replica_groups=mesh['space'=16,'chan'=2] {'chan'}, dimensions={0}, use_global_device_ids=true | all-gather | bytes 786432 | tf_op jit(solution)/shard_map/all_gather | solution.py:38
  17.9 1.3 %collective-permute-start.1 = (bf16[256,1,8,128]{0,2,3,1:T(8,128)(2,1)S(1)}, bf16[256,1,8,128]{0,2,3,1:T(8,128)(2,1)S(1)}, u32[]{:S(2)}, u32[]{:S(2)}) collective-permute-start(bf16[256,1,8,128]{0,2,3,1:T(8,128)(2,1)S(1)} %all_gather.3), channel_id=1, source_target_pairs={{2,0},{4,2},{6,4},{8,6},{10,8},{12,10},{14,12},{16,14},{18,16},{20... | collective-permute-start | bytes 1572872 | tf_op jit(solution)/shard_map/ppermute | solution.py:17
  19.2 3.1 %collective-permute-start = (bf16[256,1,8,128]{0,2,3,1:T(8,128)(2,1)S(1)}, bf16[256,1,8,128]{0,2,3,1:T(8,128)(2,1)S(1)}, u32[]{:S(2)}, u32[]{:S(2)}) collective-permute-start(bf16[256,1,8,128]{0,2,3,1:T(8,128)(2,1)S(1)} %all_gather.3), channel_id=1, source_target_pairs={{0,2},{2,4},{4,6},{6,8},{8,10},{10,12},{12,14},{14,16},{16,18},{18... | collective-permute-start | bytes 1572872 | tf_op jit(solution)/shard_map/ppermute | solution.py:15
  22.2 0.0 collective-permute-done.1
  22.2 1.5 %collective-permute-done = bf16[256,1,8,128]{0,2,3,1:T(8,128)(2,1)S(1)} collective-permute-done((bf16[256,1,8,128]{0,2,3,1:T(8,128)(2,1)S(1)}, bf16[256,1,8,128]{0,2,3,1:T(8,128)(2,1)S(1)}, u32[]{:S(2)}, u32[]{:S(2)}) %collective-permute-start) | collective-permute-done | bytes 524320 | tf_op jit(solution)/shard_map/ppermute | solution.py:15
  23.7 0.2 maximum_bitcast_fusion
  23.9 0.1 pad
  24.0 0.0 copy-start.3
  24.0 0.0 copy-start.4
  24.0 0.3 copy.17
  24.4 1.1 copy-done.3
  25.5 0.0 copy-done.4
  25.5 0.0 copy-start.2
  25.5 4.1 %fusion.10 = f32[1,8,8,17,128]{4,2,3,1,0:T(8,128)S(1)} fusion(bf16[256,3,3,3,128]{4,0,3,2,1:T(8,128)(2,1)S(1)} %bitcast.46, bf16[256,3,8,1,7,2]{0,4,5,2,1,3:T(8,128)(2,1)S(1)} %slice.4, bf16[256,3,8,1,8,17]{0,4,5,2,1,3:T(8,128)(2,1)S(1)} %copy.17, pred[8,17]{0,1:T(8,128)(4,1)S(1)} %copy-done.4), kind=kOutput, calls=%fused_computation.13 | convolution fusion | flops 1770496000 | bytes 4169864 | tf_op jit(solution)/shard_map/conv_general_dilated | solution.py:26
  29.6 0.1 copy.18
  29.7 0.0 copy-done.2
  29.7 0.1 fusion.22
  29.8 1.3 %collective-permute-start.3 = (bf16[128,1,8,128]{0,2,3,1:T(8,128)(2,1)S(1)}, bf16[128,1,8,128]{0,2,3,1:T(8,128)(2,1)S(1)}, u32[]{:S(2)}, u32[]{:S(2)}) collective-permute-start(bf16[128,1,8,128]{0,2,3,1:T(8,128)(2,1)S(1)} %fusion.22), channel_id=1, source_target_pairs={{2,0},{4,2},{6,4},{8,6},{10,8},{12,10},{14,12},{16,14},{18,16},{20... | collective-permute-start | bytes 786440 | tf_op jit(solution)/shard_map/ppermute | solution.py:17
  31.1 12.4 %collective-permute-start.2 = (bf16[128,1,8,128]{0,2,3,1:T(8,128)(2,1)S(1)}, bf16[128,1,8,128]{0,2,3,1:T(8,128)(2,1)S(1)}, u32[]{:S(2)}, u32[]{:S(2)}) collective-permute-start(bf16[128,1,8,128]{0,2,3,1:T(8,128)(2,1)S(1)} %fusion.22), channel_id=1, source_target_pairs={{0,2},{2,4},{4,6},{6,8},{8,10},{10,12},{12,14},{14,16},{16,18},{18... | collective-permute-start | bytes 786440 | tf_op jit(solution)/shard_map/ppermute | solution.py:15
  43.5 0.0 collective-permute-done.3
  43.5 0.9 collective-permute-done.2
  44.5 0.1 maximum_bitcast_fusion.1
  44.6 0.1 pad.2
  44.6 0.1 copy.20
  44.8 0.0 copy-done
  44.8 2.2 %fusion.9 = bf16[1,8,8,17,256]{4,2,3,1,0:T(8,128)(2,1)S(1)} fusion(bf16[128,3,3,3,256]{4,0,3,2,1:T(8,128)(2,1)S(1)} %bitcast.39, bf16[128,3,8,1,7,2]{0,4,5,2,1,3:T(8,128)(2,1)S(1)} %slice.6, bf16[128,3,8,1,8,17]{0,4,5,2,1,3:T(8,128)(2,1)S(1)} %copy.20, pred[8,17]{0,1:T(8,128)(4,1)S(1)} %copy-done.4), kind=kOutput, calls=%fused_computation.12 | convolution fusion | flops 1768112128 | bytes 3248264 | tf_op jit(solution)/shard_map/conv_general_dilated | solution.py:26
  47.0 0.1 copy.21
  47.1 11.8 %copy.23 = bf16[256,1,8,128]{2,3,1,0:T(8,128)(2,1)} copy(bf16[256,1,8,128]{0,2,3,1:T(8,128)(2,1)S(1)} %slice_bitcast_fusion) | data formatting | bytes 1048576
  58.9 13.5 %reshape.71 = bf16[256,1024]{1,0:T(8,128)(2,1)} reshape(bf16[256,1,128,8]{3,2,1,0:T(8,128)(2,1)} %bitcast.40) | data formatting | bytes 1048576
  72.4 0.0 reduce-scatter.4.cloned.1.call-update
  72.4 21.3 %reduce-scatter.4.cloned.1.call-done = bf16[128,1024]{1,0:T(8,128)(2,1)} async-done(((bf16[256,1024]{1,0:T(8,128)(2,1)}), bf16[128,1024]{1,0:T(8,128)(2,1)}) %reduce-scatter.4.cloned.1.call-update) | async-done | bytes 262160
  93.8 6.8 %reshape.72 = bf16[128,1,128,8]{3,2,1,0:T(8,128)(2,1)} reshape(bf16[128,1024]{1,0:T(8,128)(2,1)} %reduce-scatter.4.cloned.1.call-done) | data formatting | bytes 524288
  100.6 0.0 copy-start.1
  100.6 5.5 %copy.24 = bf16[128,1,8,128]{0,2,3,1:T(8,128)(2,1)S(1)} copy(bf16[128,1,8,128]{2,3,1,0:T(8,128)(2,1)} %bitcast.41) | data formatting | bytes 524288
  106.1 0.0 copy-done.1
  106.1 0.1 maximum_convert_fusion
  106.2 0.9 copy.22
  (3 shorter events, 0.1 us)
Async XLA Ops:
  6.5 38.3 %copy-start = (bf16[128,27,256]{2,0,1:T(8,128)(2,1)S(1)}, bf16[128,27,256]{2,0,1:T(8,128)(2,1)}, u32[]{:S(2)}) copy-start(bf16[128,27,256]{2,0,1:T(8,128)(2,1)} %param.8) | copy-start | bytes 5308420
  6.5 87.2 %reduce-scatter.4.cloned.1.call-start = ((), (), s32[]{:S(2)}) async-start(), calls=%async_computation.1 | async-start | bytes 786432
  17.9 4.4 %collective-permute-start.1 = (bf16[256,1,8,128]{0,2,3,1:T(8,128)(2,1)S(1)}, bf16[256,1,8,128]{0,2,3,1:T(8,128)(2,1)S(1)}, u32[]{:S(2)}, u32[]{:S(2)}) collective-permute-start(bf16[256,1,8,128]{0,2,3,1:T(8,128)(2,1)S(1)} %all_gather.3), channel_id=1, source_target_pairs={{2,0},{4,2},{6,4},{8,6},{10,8},{12,10},{14,12},{16,14},{18,16},{20... | collective-permute-start | bytes 1572872 | tf_op jit(solution)/shard_map/ppermute | solution.py:17
  19.2 4.6 %collective-permute-start = (bf16[256,1,8,128]{0,2,3,1:T(8,128)(2,1)S(1)}, bf16[256,1,8,128]{0,2,3,1:T(8,128)(2,1)S(1)}, u32[]{:S(2)}, u32[]{:S(2)}) collective-permute-start(bf16[256,1,8,128]{0,2,3,1:T(8,128)(2,1)S(1)} %all_gather.3), channel_id=1, source_target_pairs={{0,2},{2,4},{4,6},{6,8},{8,10},{10,12},{12,14},{14,16},{16,18},{18... | collective-permute-start | bytes 1572872 | tf_op jit(solution)/shard_map/ppermute | solution.py:15
  24.0 1.5 %copy-start.3 = (bf16[256,27,128]{2,0,1:T(8,128)(2,1)S(1)}, bf16[256,27,128]{2,0,1:T(8,128)(2,1)}, u32[]{:S(2)}) copy-start(bf16[256,27,128]{2,0,1:T(8,128)(2,1)} %param.6) | copy-start | bytes 5308420
  24.0 1.5 %copy-start.4 = (pred[8,17]{0,1:T(8,128)(4,1)S(1)}, pred[8,17]{0,1:T(8,128)(4,1)}, u32[]{:S(2)}) copy-start(pred[8,17]{0,1:T(8,128)(4,1)} %constant.13) | copy-start | bytes 412
  25.5 4.2 %copy-start.2 = (f32[128]{0:T(128)S(1)}, f32[128]{0:T(128)}, u32[]{:S(2)}) copy-start(f32[128]{0:T(128)} %param.7) | copy-start | bytes 1540
  29.8 13.7 %collective-permute-start.3 = (bf16[128,1,8,128]{0,2,3,1:T(8,128)(2,1)S(1)}, bf16[128,1,8,128]{0,2,3,1:T(8,128)(2,1)S(1)}, u32[]{:S(2)}, u32[]{:S(2)}) collective-permute-start(bf16[128,1,8,128]{0,2,3,1:T(8,128)(2,1)S(1)} %fusion.22), channel_id=1, source_target_pairs={{2,0},{4,2},{6,4},{8,6},{10,8},{12,10},{14,12},{16,14},{18,16},{20... | collective-permute-start | bytes 786440 | tf_op jit(solution)/shard_map/ppermute | solution.py:17
  31.1 13.4 %collective-permute-start.2 = (bf16[128,1,8,128]{0,2,3,1:T(8,128)(2,1)S(1)}, bf16[128,1,8,128]{0,2,3,1:T(8,128)(2,1)S(1)}, u32[]{:S(2)}, u32[]{:S(2)}) collective-permute-start(bf16[128,1,8,128]{0,2,3,1:T(8,128)(2,1)S(1)} %fusion.22), channel_id=1, source_target_pairs={{0,2},{2,4},{4,6},{6,8},{8,10},{10,12},{12,14},{14,16},{16,18},{18... | collective-permute-start | bytes 786440 | tf_op jit(solution)/shard_map/ppermute | solution.py:15
  100.6 5.5 %copy-start.1 = (f32[128]{0:T(128)S(1)}, f32[128]{0:T(128)}, u32[]{:S(2)}) copy-start(f32[128]{0:T(128)} %param.9) | copy-start | bytes 1540
Sparse Core Ops, SparseCore 0:
  72.5 21.1 reduce-scatter.3
where the time goes:
time: 114 us
  local copies, waits for them, and re-layouts  41.9 us (37%)
  waiting for transfers between devices  23.8 us (21%)
  starting transfers between devices  18.1 us (16%)
  between operations  13.6 us (12%)
  blocking collectives  9.98 us (9%)
  matrix products  6.29 us (6%)
    unnamed x15, local copies, waits for them, and re-layouts  40 us
    unnamed x2, waiting for transfers between devices  21.4 us
    ppermute x2, starting transfers between devices, with_halo(): lax.ppermute(tail, axis, [(i, (i + 1) % count) for i in range(ends)])  15.5 us
    all_gather x1, blocking collectives, per_device(): gathered = lax.all_gather(volume, 'chan', axis=0, tiled=True)  9.98 us
    conv_general_dilated x2, matrix products, apply_taps(): lax.conv_general_dilated(slab[None], kernel, (1, 1, 1), [(0, 0), (row_pad...  6.29 us
    ppermute x2, starting transfers between devices, with_halo(): lax.ppermute(head, axis, [((i + 1) % count, i) for i in range(ends)])  2.57 us
    ppermute x2, waiting for transfers between devices, with_halo(): lax.ppermute(tail, axis, [(i, (i + 1) % count) for i in range(ends)])  2.41 us
  transfers between devices with their start and end apart: 5, of which 3 were waited for; matrix products, arithmetic and copies ran while one was open for 0% of the time, Pallas kernels for 0%

commit v1 on v0

--- a/solution.py
+++ b/solution.py
@@ -2,6 +2,18 @@
 import jax.numpy as jnp
 from jax import lax
 from jax.sharding import PartitionSpec as P
+
+
+def collect(array, axis, dim):
+    ways, here, lap = (lax.axis_size(axis), lax.axis_index(axis), array.shape[dim])
+    line, have = (array, 1)
+    while have < ways:
+        line = jnp.concatenate(
+            [line, lax.ppermute(line, axis, [(d, (d - have) % ways) for d in range(ways)])],
+            axis=dim,
+        )
+        have = 2 * have
+    return jnp.roll(line, here * lap, axis=dim)
 
 
 def with_halo(cells, sides, width):
@@ -35,7 +47,7 @@
 
 
 def per_device(volume, w_first, b_first, w_second, b_second):
-    gathered = lax.all_gather(volume, "chan", axis=0, tiled=True)
+    gathered = collect(volume, "chan", 0)
     framed = with_halo(gathered, (("space", 1),), 1)
     first_sum = apply_taps(framed, w_first, 1)
     hidden = jax.nn.relu(first_sum + b_first[:, None, None, None]).astype(jnp.bfloat16)

time: 114 us -> 114 us (level)
  blocking collectives: 9.98 us -> 0 us
  waiting for transfers between devices: 23.8 us -> 30.1 us
  starting transfers between devices: 18.1 us -> 21.1 us
    all_gather x1 -> x0, blocking collectives: 9.98 us -> none  [per_device(): gathered = lax.all_gather(volume, 'chan', axis=0, tiled=True)]
    ppermute x0 -> x1, waiting for transfers between devices: none -> 6.31 us  [collect(): lax.ppermute(line, axis, [(d, (d - have) % ways) for d in range(ways)])]
    ppermute x0 -> x1, starting transfers between devices: none -> 3.03 us  [collect(): lax.ppermute(line, axis, [(d, (d - have) % ways) for d in range(ways)])]
  transfers between devices with their start and end apart: 5 -> 6, of which waited for: 3 -> 4; matrix products, arithmetic and copies ran while one was open for 0% -> 0% of each run, Pallas kernels for 0% -> 0%
where the time goes in v1:
time: 114 us
  local copies, waits for them, and re-layouts  41.8 us (37%)
  waiting for transfers between devices  30.1 us (26%)
  starting transfers between devices  21.1 us (19%)
  between operations  13.6 us (12%)
  matrix products  6.29 us (6%)
    unnamed x15, local copies, waits for them, and re-layouts  40 us
    unnamed x2, waiting for transfers between devices  21.4 us
    ppermute x2, starting transfers between devices, with_halo(): lax.ppermute(tail, axis, [(i, (i + 1) % count) for i in range(ends)])  15.5 us
    ppermute x1, waiting for transfers between devices, collect(): lax.ppermute(line, axis, [(d, (d - have) % ways) for d in range(ways)])  6.31 us
    conv_general_dilated x2, matrix products, apply_taps(): lax.conv_general_dilated(slab[None], kernel, (1, 1, 1), [(0, 0), (row_pad...  6.29 us
    ppermute x1, starting transfers between devices, collect(): lax.ppermute(line, axis, [(d, (d - have) % ways) for d in range(ways)])  3.03 us
    ppermute x2, starting transfers between devices, with_halo(): lax.ppermute(head, axis, [((i + 1) % count, i) for i in range(ends)])  2.58 us
    ppermute x2, waiting for transfers between devices, with_halo(): lax.ppermute(tail, axis, [(i, (i + 1) % count) for i in range(ends)])  2.41 us
  transfers between devices with their start and end apart: 6, of which 4 were waited for; matrix products, arithmetic and copies ran while one was open for 0% of the time, Pallas kernels for 0%

profile of v1, /device:TPU:0, one launch (start us, length us, event | category | flops | bytes accessed | tf_op | source)
XLA Modules:
  0.0 113.7 jit_solution(12312533679840645471)
XLA Ops:
  6.5 0.0 copy-start
  6.5 0.0 reduce-scatter.4.cloned.1.call-start
  6.5 1.3 %copy.18 = bf16[128,1,8,128]{0,2,3,1:T(8,128)(2,1)S(1)} copy(bf16[128,1,8,128]{3,2,1,0:T(8,128)(2,1)} %param.5) | data formatting | bytes 524288 | tf_op args[0]
  7.9 3.0 %collective-permute-start = (bf16[128,1,8,128]{0,2,3,1:T(8,128)(2,1)S(1)}, bf16[128,1,8,128]{0,2,3,1:T(8,128)(2,1)S(1)}, u32[]{:S(2)}, u32[]{:S(2)}) collective-permute-start(bf16[128,1,8,128]{0,2,3,1:T(8,128)(2,1)S(1)} %copy.18), channel_id=1, source_target_pairs={{0,1},{1,0},{2,3},{3,2},{4,5},{5,4},{6,7},{7,6},{8,9},{9,8},{10,11... | collective-permute-start | bytes 786440 | tf_op jit(solution)/shard_map/ppermute | solution.py:12
  10.9 6.3 %collective-permute-done = bf16[128,1,8,128]{0,2,3,1:T(8,128)(2,1)S(1)} collective-permute-done((bf16[128,1,8,128]{0,2,3,1:T(8,128)(2,1)S(1)}, bf16[128,1,8,128]{0,2,3,1:T(8,128)(2,1)S(1)}, u32[]{:S(2)}, u32[]{:S(2)}) %collective-permute-start) | collective-permute-done | bytes 262176 | tf_op jit(solution)/shard_map/ppermute | solution.py:12
  17.2 0.4 fusion.22
  17.6 1.3 %collective-permute-start.2 = (bf16[256,1,8,128]{0,2,3,1:T(8,128)(2,1)S(1)}, bf16[256,1,8,128]{0,2,3,1:T(8,128)(2,1)S(1)}, u32[]{:S(2)}, u32[]{:S(2)}) collective-permute-start(bf16[256,1,8,128]{0,2,3,1:T(8,128)(2,1)S(1)} %fusion.22), channel_id=1, source_target_pairs={{2,0},{4,2},{6,4},{8,6},{10,8},{12,10},{14,12},{16,14},{18,16},{20... | collective-permute-start | bytes 1572872 | tf_op jit(solution)/shard_map/ppermute | solution.py:29
  18.9 3.1 %collective-permute-start.1 = (bf16[256,1,8,128]{0,2,3,1:T(8,128)(2,1)S(1)}, bf16[256,1,8,128]{0,2,3,1:T(8,128)(2,1)S(1)}, u32[]{:S(2)}, u32[]{:S(2)}) collective-permute-start(bf16[256,1,8,128]{0,2,3,1:T(8,128)(2,1)S(1)} %fusion.22), channel_id=1, source_target_pairs={{0,2},{2,4},{4,6},{6,8},{8,10},{10,12},{12,14},{14,16},{16,18},{18... | collective-permute-start | bytes 1572872 | tf_op jit(solution)/shard_map/ppermute | solution.py:27
  22.0 0.0 collective-permute-done.2
  22.0 1.5 %collective-permute-done.1 = bf16[256,1,8,128]{0,2,3,1:T(8,128)(2,1)S(1)} collective-permute-done((bf16[256,1,8,128]{0,2,3,1:T(8,128)(2,1)S(1)}, bf16[256,1,8,128]{0,2,3,1:T(8,128)(2,1)S(1)}, u32[]{:S(2)}, u32[]{:S(2)}) %collective-permute-start.1) | collective-permute-done | bytes 524320 | tf_op jit(solution)/shard_map/ppermute | solution.py:27
  23.5 0.2 maximum_bitcast_fusion
  23.7 0.1 pad
  23.8 0.0 copy-start.3
  23.8 0.0 copy-start.4
  23.8 0.3 copy.21
  24.2 1.1 copy-done.3
  25.3 0.0 copy-done.4
  25.3 0.0 copy-start.2
  25.3 4.1 %fusion.10 = f32[1,8,8,17,128]{4,2,3,1,0:T(8,128)S(1)} fusion(bf16[256,3,3,3,128]{4,0,3,2,1:T(8,128)(2,1)S(1)} %bitcast.46, bf16[256,3,8,1,7,2]{0,4,5,2,1,3:T(8,128)(2,1)S(1)} %slice.4, bf16[256,3,8,1,8,17]{0,4,5,2,1,3:T(8,128)(2,1)S(1)} %copy.21, pred[8,17]{0,1:T(8,128)(4,1)S(1)} %copy-done.4), kind=kOutput, calls=%fused_computation.13 | convolution fusion | flops 1770496000 | bytes 4169864 | tf_op jit(solution)/shard_map/conv_general_dilated | solution.py:38
  29.4 0.1 copy.22
  29.5 0.0 copy-done.2
  29.5 0.1 fusion.25
  29.6 1.3 %collective-permute-start.4 = (bf16[128,1,8,128]{0,2,3,1:T(8,128)(2,1)S(1)}, bf16[128,1,8,128]{0,2,3,1:T(8,128)(2,1)S(1)}, u32[]{:S(2)}, u32[]{:S(2)}) collective-permute-start(bf16[128,1,8,128]{0,2,3,1:T(8,128)(2,1)S(1)} %fusion.25), channel_id=1, source_target_pairs={{2,0},{4,2},{6,4},{8,6},{10,8},{12,10},{14,12},{16,14},{18,16},{20... | collective-permute-start | bytes 786440 | tf_op jit(solution)/shard_map/ppermute | solution.py:29
  30.9 12.4 %collective-permute-start.3 = (bf16[128,1,8,128]{0,2,3,1:T(8,128)(2,1)S(1)}, bf16[128,1,8,128]{0,2,3,1:T(8,128)(2,1)S(1)}, u32[]{:S(2)}, u32[]{:S(2)}) collective-permute-start(bf16[128,1,8,128]{0,2,3,1:T(8,128)(2,1)S(1)} %fusion.25), channel_id=1, source_target_pairs={{0,2},{2,4},{4,6},{6,8},{8,10},{10,12},{12,14},{14,16},{16,18},{18... | collective-permute-start | bytes 786440 | tf_op jit(solution)/shard_map/ppermute | solution.py:27
  43.3 0.0 collective-permute-done.4
  43.3 0.9 collective-permute-done.3
  44.3 0.1 maximum_bitcast_fusion.1
  44.4 0.1 pad.2
  44.4 0.1 copy.24
  44.6 0.0 copy-done
  44.6 2.2 %fusion.9 = bf16[1,8,8,17,256]{4,2,3,1,0:T(8,128)(2,1)S(1)} fusion(bf16[128,3,3,3,256]{4,0,3,2,1:T(8,128)(2,1)S(1)} %bitcast.39, bf16[128,3,8,1,7,2]{0,4,5,2,1,3:T(8,128)(2,1)S(1)} %slice.6, bf16[128,3,8,1,8,17]{0,4,5,2,1,3:T(8,128)(2,1)S(1)} %copy.24, pred[8,17]{0,1:T(8,128)(4,1)S(1)} %copy-done.4), kind=kOutput, calls=%fused_computation.12 | convolution fusion | flops 1768112128 | bytes 3248264 | tf_op jit(solution)/shard_map/conv_general_dilated | solution.py:38
  46.8 0.1 copy.25
  46.9 11.8 %copy.27 = bf16[256,1,8,128]{2,3,1,0:T(8,128)(2,1)} copy(bf16[256,1,8,128]{0,2,3,1:T(8,128)(2,1)S(1)} %slice_bitcast_fusion) | data formatting | bytes 1048576
  58.7 13.5 %reshape.71 = bf16[256,1024]{1,0:T(8,128)(2,1)} reshape(bf16[256,1,128,8]{3,2,1,0:T(8,128)(2,1)} %bitcast.40) | data formatting | bytes 1048576
  72.2 0.0 reduce-scatter.4.cloned.1.call-update
  72.2 21.4 %reduce-scatter.4.cloned.1.call-done = bf16[128,1024]{1,0:T(8,128)(2,1)} async-done(((bf16[256,1024]{1,0:T(8,128)(2,1)}), bf16[128,1024]{1,0:T(8,128)(2,1)}) %reduce-scatter.4.cloned.1.call-update) | async-done | bytes 262160
  93.6 6.8 %reshape.72 = bf16[128,1,128,8]{3,2,1,0:T(8,128)(2,1)} reshape(bf16[128,1024]{1,0:T(8,128)(2,1)} %reduce-scatter.4.cloned.1.call-done) | data formatting | bytes 524288
  100.4 0.0 copy-start.1
  100.4 5.5 %copy.28 = bf16[128,1,8,128]{0,2,3,1:T(8,128)(2,1)S(1)} copy(bf16[128,1,8,128]{2,3,1,0:T(8,128)(2,1)} %bitcast.41) | data formatting | bytes 524288
  105.9 0.0 copy-done.1
  105.9 0.1 maximum_convert_fusion
  106.0 0.9 copy.26
  (3 shorter events, 0.1 us)
Async XLA Ops:
  6.5 38.0 %copy-start = (bf16[128,27,256]{2,0,1:T(8,128)(2,1)S(1)}, bf16[128,27,256]{2,0,1:T(8,128)(2,1)}, u32[]{:S(2)}) copy-start(bf16[128,27,256]{2,0,1:T(8,128)(2,1)} %param.8) | copy-start | bytes 5308420
  6.5 87.0 %reduce-scatter.4.cloned.1.call-start = ((), (), s32[]{:S(2)}) async-start(), calls=%async_computation.1 | async-start | bytes 786432
  7.9 9.3 %collective-permute-start = (bf16[128,1,8,128]{0,2,3,1:T(8,128)(2,1)S(1)}, bf16[128,1,8,128]{0,2,3,1:T(8,128)(2,1)S(1)}, u32[]{:S(2)}, u32[]{:S(2)}) collective-permute-start(bf16[128,1,8,128]{0,2,3,1:T(8,128)(2,1)S(1)} %copy.18), channel_id=1, source_target_pairs={{0,1},{1,0},{2,3},{3,2},{4,5},{5,4},{6,7},{7,6},{8,9},{9,8},{10,11... | collective-permute-start | bytes 786440 | tf_op jit(solution)/shard_map/ppermute | solution.py:12
  17.6 4.4 %collective-permute-start.2 = (bf16[256,1,8,128]{0,2,3,1:T(8,128)(2,1)S(1)}, bf16[256,1,8,128]{0,2,3,1:T(8,128)(2,1)S(1)}, u32[]{:S(2)}, u32[]{:S(2)}) collective-permute-start(bf16[256,1,8,128]{0,2,3,1:T(8,128)(2,1)S(1)} %fusion.22), channel_id=1, source_target_pairs={{2,0},{4,2},{6,4},{8,6},{10,8},{12,10},{14,12},{16,14},{18,16},{20... | collective-permute-start | bytes 1572872 | tf_op jit(solution)/shard_map/ppermute | solution.py:29
  18.9 4.6 %collective-permute-start.1 = (bf16[256,1,8,128]{0,2,3,1:T(8,128)(2,1)S(1)}, bf16[256,1,8,128]{0,2,3,1:T(8,128)(2,1)S(1)}, u32[]{:S(2)}, u32[]{:S(2)}) collective-permute-start(bf16[256,1,8,128]{0,2,3,1:T(8,128)(2,1)S(1)} %fusion.22), channel_id=1, source_target_pairs={{0,2},{2,4},{4,6},{6,8},{8,10},{10,12},{12,14},{14,16},{16,18},{18... | collective-permute-start | bytes 1572872 | tf_op jit(solution)/shard_map/ppermute | solution.py:27
  23.8 1.5 %copy-start.3 = (bf16[256,27,128]{2,0,1:T(8,128)(2,1)S(1)}, bf16[256,27,128]{2,0,1:T(8,128)(2,1)}, u32[]{:S(2)}) copy-start(bf16[256,27,128]{2,0,1:T(8,128)(2,1)} %param.6) | copy-start | bytes 5308420
  23.8 1.5 %copy-start.4 = (pred[8,17]{0,1:T(8,128)(4,1)S(1)}, pred[8,17]{0,1:T(8,128)(4,1)}, u32[]{:S(2)}) copy-start(pred[8,17]{0,1:T(8,128)(4,1)} %constant.41) | copy-start | bytes 412
  25.3 4.2 %copy-start.2 = (f32[128]{0:T(128)S(1)}, f32[128]{0:T(128)}, u32[]{:S(2)}) copy-start(f32[128]{0:T(128)} %param.7) | copy-start | bytes 1540
  29.6 13.7 %collective-permute-start.4 = (bf16[128,1,8,128]{0,2,3,1:T(8,128)(2,1)S(1)}, bf16[128,1,8,128]{0,2,3,1:T(8,128)(2,1)S(1)}, u32[]{:S(2)}, u32[]{:S(2)}) collective-permute-start(bf16[128,1,8,128]{0,2,3,1:T(8,128)(2,1)S(1)} %fusion.25), channel_id=1, source_target_pairs={{2,0},{4,2},{6,4},{8,6},{10,8},{12,10},{14,12},{16,14},{18,16},{20... | collective-permute-start | bytes 786440 | tf_op jit(solution)/shard_map/ppermute | solution.py:29
  30.9 13.4 %collective-permute-start.3 = (bf16[128,1,8,128]{0,2,3,1:T(8,128)(2,1)S(1)}, bf16[128,1,8,128]{0,2,3,1:T(8,128)(2,1)S(1)}, u32[]{:S(2)}, u32[]{:S(2)}) collective-permute-start(bf16[128,1,8,128]{0,2,3,1:T(8,128)(2,1)S(1)} %fusion.25), channel_id=1, source_target_pairs={{0,2},{2,4},{4,6},{6,8},{8,10},{10,12},{12,14},{14,16},{16,18},{18... | collective-permute-start | bytes 786440 | tf_op jit(solution)/shard_map/ppermute | solution.py:27
  100.4 5.5 %copy-start.1 = (f32[128]{0:T(128)S(1)}, f32[128]{0:T(128)}, u32[]{:S(2)}) copy-start(f32[128]{0:T(128)} %param.9) | copy-start | bytes 1540
Sparse Core Ops, SparseCore 0:
  72.3 21.2 reduce-scatter.3
